TPU v7x, 512 devices: a whole 4x8x8 slice. The times are simulated.
512 devices in a mesh: section: 8 (over z), tok: 64 (over y, x, core).
Axes of the slice: x: 4, y: 8, z: 8, core: 2. Of those that a mesh axis runs over, the one named last changes fastest.
Arguments:
- queries: bfloat16 [8, 16384, 4096], P('section', 'tok'), may hold values from -120 to 120
- suffix_kv: bfloat16 [8, 16384, 1024], P('section', 'tok'), may hold values from -4 to 4
- prefix_kv: bfloat16 [8, 64, 64, 1024], P('section', 'tok'), may hold values from -4 to 4
- served: int32 [8, 128, 8], P('section'), may hold values from -1 to 63, as said below
Outputs:
- passed: bfloat16 [8, 16384, 4096], P('section', 'tok')
Inputs may be any that keep to these rules, and one draw needn't show every extreme that they name: `served`: entry k of a row is -1 or a page in [k * 8, (k + 1) * 8); live entries come first, then -1; entry 0 is always live, and block 0 of every section has all 8 live.
All inputs are finite; a program needn't handle non-finite values.
Results may differ from a plain program's by a relative error of at most 0.0029.
Values may be sent and summed in bfloat16 or wider, within the bound.
No kernel may reach another device: no remote copies, remote signals or barrier semaphores. Data moves between devices by JAX's collectives and lax.ppermute only.
A program may use at most 64 MiB of HBM per device.

v0:
```python
import math

import jax
import jax.numpy as jnp
from jax import lax
from jax.sharding import PartitionSpec as P

Q_HEADS = 32
KV_HEADS = 4
HEAD = 128
BLOCK = 128
PAGE = 64
QB_DEV = 2
DEPTH = 8


def from_behind(x, axis, by):
    devices = lax.axis_size(axis)
    return lax.ppermute(x, axis, [(i, (i + by) % devices) for i in range(devices)])


def attend(query_rows, key_rows, value_rows, allowed, score_scale):
    scores = (
        jnp.einsum("qgd,kd->gqk", query_rows, key_rows, preferred_element_type=jnp.float32)
        * score_scale
    )
    scores = jnp.where(allowed[None], scores, -jnp.inf)
    row_top = jnp.max(scores, axis=2, keepdims=True)
    exponent = jnp.exp(scores - row_top)
    totals = jnp.sum(exponent, axis=2)
    weights = exponent.astype(jnp.bfloat16)
    mixture = jnp.einsum("gqk,kd->qgd", weights, value_rows, preferred_element_type=jnp.float32)
    return (mixture / jnp.transpose(totals)[:, :, None]).astype(jnp.bfloat16)


def on_device(queries, suffix_kv, prefix_kv, served):
    my_index = lax.axis_index("tok")
    group_size = Q_HEADS // KV_HEADS
    score_scale = 1.0 / math.sqrt(HEAD)
    first_block = my_index * QB_DEV
    my_served = lax.dynamic_slice_in_dim(served[0], first_block, QB_DEV, 0)
    complete = lax.all_gather(prefix_kv, "tok", axis=1, tiled=True)
    chosen = complete[0][jnp.maximum(my_served, 0)]
    prefix_pairs = chosen.reshape(QB_DEV, DEPTH * PAGE, 2, KV_HEADS, HEAD)
    own_pairs = suffix_kv[0].reshape(QB_DEV, BLOCK, 2, KV_HEADS, HEAD)
    query_blocks = queries[0].reshape(QB_DEV, BLOCK, KV_HEADS, group_size, HEAD)
    live_rows = jnp.broadcast_to((my_served >= 0)[:, :, None], (QB_DEV, DEPTH, PAGE))
    live_rows = live_rows.reshape(QB_DEV, DEPTH * PAGE)
    row_index = lax.broadcasted_iota(jnp.int32, (BLOCK, BLOCK), 0)
    col_index = lax.broadcasted_iota(jnp.int32, (BLOCK, BLOCK), 1)
    causal = col_index <= row_index

    def per_item(position):
        block_id = position // KV_HEADS
        head_id = position % KV_HEADS
        key_rows = jnp.concatenate(
            [prefix_pairs[block_id, :, 0, head_id], own_pairs[block_id, :, 0, head_id]], axis=0
        )
        value_rows = jnp.concatenate(
            [prefix_pairs[block_id, :, 1, head_id], own_pairs[block_id, :, 1, head_id]], axis=0
        )
        allowed = jnp.concatenate(
            [jnp.broadcast_to(live_rows[block_id][None], (BLOCK, DEPTH * PAGE)), causal], axis=1
        )
        return attend(
            query_blocks[block_id, :, head_id], key_rows, value_rows, allowed, score_scale
        )

    results = lax.map(per_item, jnp.arange(QB_DEV * KV_HEADS))
    results = results.reshape(QB_DEV, KV_HEADS, BLOCK, group_size * HEAD)
    attention = jnp.transpose(results, (0, 2, 1, 3)).reshape(1, QB_DEV * BLOCK, Q_HEADS * HEAD)
    return from_behind(attention, "section", 1)


def solution(mesh):
    placed = (
        P("section", "tok", None),
        P("section", "tok", None),
        P("section", "tok", None, None),
        P("section", None, None),
    )
    return jax.shard_map(
        on_device, mesh=mesh, in_specs=placed, out_specs=P("section", "tok", None), check_vma=False
    )
```

profile of v0, /device:TPU:1, one launch (start us, length us, event | category | flops | bytes accessed | tf_op | source)
XLA Modules:
  0.0 245.5 jit_solution(2177986282207942858)
XLA Ops:
  9.2 3.5 %copy.32 = bf16[32,8,32,128]{3,2,1,0:T(8,128)(2,1)} copy(bf16[32,8,32,128]{3,1,2,0:T(8,128)(2,1)} %bitcast.89) | data formatting | bytes 4194304
  13.2 91.7 %all-gather.2.cloned.1.call-done = bf16[1,64,64,1024]{3,2,0,1:T(8,128)(2,1)} async-done(((bf16[1,1,64,1024]{3,2,0,1:T(8,128)(2,1)}), bf16[1,64,64,1024]{3,2,0,1:T(8,128)(2,1)}) %all-gather.2.cloned.1.call-update) | async-done | bytes 8388624 | tf_op jit(solution)/shard_map/all_gather | solution.py:42
  104.8 4.1 %gather_fusion = bf16[16,64,1024]{2,1,0:T(8,128)(2,1)S(1)} fusion(bf16[64,64,1024]{2,1,0:T(8,128)(2,1)} %bitcast.92, s32[1024]{0:T(1024)S(1)} %pad_clamp_fusion), kind=kCustom, calls=%fused_computation | custom fusion | bytes 4194368 | tf_op jit(solution)/shard_map/gather | solution.py:43
  108.9 2.7 %reshape.35 = bf16[2,512,2,4,128]{4,3,2,1,0:T(4,128)(2,1)} reshape(bf16[16,64,1024]{2,1,0:T(8,128)(2,1)S(1)} %gather_fusion) | data formatting | bytes 4194304 | tf_op jit(solution)/shard_map/reshape | solution.py:44
  111.6 3.3 %copy.26 = bf16[2,512,2,4,128]{4,1,3,2,0:T(8,128)(2,1)} copy(bf16[2,512,2,4,128]{4,3,2,1,0:T(4,128)(2,1)} %reshape.35) | data formatting | bytes 4194304
  115.0 64.8 %while.13 = (s32[]{:T(128)}, bf16[8,128,8,128]{1,3,2,0:T(8,128)(2,1)}, s32[8]{0:T(128)S(1)}, bf16[2,512,2,4,128]{4,1,3,2,0:T(8,128)(2,1)}, bf16[2,128,2,4,128]{4...) while((s32[]{:T(128)}, ...), condition=%wide.region_3.4_spmd.clone, body=%wide.region_0.3_spmd.clone.sunk | while | flops 343767072 | bytes 10608301 | solution.py:69
  118.0 1.0 constant_dynamic-slice_fusion.8
  119.0 1.0 constant_dynamic-slice_fusion.6
  121.6 1.5 fusion.39
  126.1 1.0 constant_dynamic-slice_fusion.8
  127.1 1.0 constant_dynamic-slice_fusion.6
  129.7 1.5 fusion.39
  134.2 1.0 constant_dynamic-slice_fusion.8
  135.2 1.0 constant_dynamic-slice_fusion.6
  137.8 1.5 fusion.39
  142.3 1.0 constant_dynamic-slice_fusion.8
  143.3 1.0 constant_dynamic-slice_fusion.6
  145.9 1.5 fusion.39
  150.4 1.0 constant_dynamic-slice_fusion.8
  154.0 1.5 fusion.39
  158.5 1.0 constant_dynamic-slice_fusion.8
  159.5 1.0 constant_dynamic-slice_fusion.6
  162.1 1.5 fusion.39
  166.6 1.0 constant_dynamic-slice_fusion.8
  170.2 1.5 fusion.39
  174.8 1.0 constant_dynamic-slice_fusion.8
  178.3 1.5 fusion.39
  179.8 3.4 %copy.29 = bf16[2,4,128,1024]{3,1,2,0:T(4,128)(2,1)S(1)} copy(bf16[2,4,128,1024]{2,3,1,0:T(8,128)(2,1)} %bitcast.90) | data formatting | bytes 4194304 | tf_op jit(solution)/shard_map/reshape | solution.py:70
  183.1 2.8 %reshape.38 = bf16[1,256,4096]{2,1,0:T(8,128)(2,1)} reshape(bf16[2,128,4,1024]{3,2,1,0:T(4,128)(2,1)S(1)} %bitcast.87) | data formatting | bytes 4194304 | tf_op jit(solution)/shard_map/reshape | solution.py:71
  185.9 3.3 %collective-permute-start = (bf16[1,256,4096]{2,1,0:T(8,128)(2,1)}, bf16[1,256,4096]{2,1,0:T(8,128)(2,1)S(1)}, u32[]{:S(2)}, u32[]{:S(2)}) collective-permute-start(bf16[1,256,4096]{2,1,0:T(8,128)(2,1)} %reshape.38), channel_id=1, source_target_pairs={{0,64},{64,128},{128,192},{192,256},{256,320},{320,384},{384,448},... | collective-permute-start | bytes 6291464 | tf_op jit(solution)/shard_map/ppermute | solution.py:19
  189.2 48.2 %collective-permute-done = bf16[1,256,4096]{2,1,0:T(8,128)(2,1)S(1)} collective-permute-done((bf16[1,256,4096]{2,1,0:T(8,128)(2,1)}, bf16[1,256,4096]{2,1,0:T(8,128)(2,1)S(1)}, u32[]{:S(2)}, u32[]{:S(2)}) %collective-permute-start) | collective-permute-done | bytes 2097184 | tf_op jit(solution)/shard_map/ppermute | solution.py:19
  237.4 1.3 copy.51
  (99 shorter events, 23.0 us)
Async XLA Ops:
  6.5 6.2 %copy-start = (bf16[1,256,1024]{2,1,0:T(8,128)(2,1)S(1)}, bf16[1,256,1024]{2,1,0:T(8,128)(2,1)}, u32[]{:S(2)}) copy-start(bf16[1,256,1024]{2,1,0:T(8,128)(2,1)} %param.7) | copy-start | bytes 1572868
  6.5 98.3 %all-gather.2.cloned.1.call-start = ((), (), s32[]{:S(2)}) async-start(), calls=%async_computation | async-start | bytes 8519680 | tf_op jit(solution)/shard_map/all_gather | solution.py:42
  185.9 51.5 %collective-permute-start = (bf16[1,256,4096]{2,1,0:T(8,128)(2,1)}, bf16[1,256,4096]{2,1,0:T(8,128)(2,1)S(1)}, u32[]{:S(2)}, u32[]{:S(2)}) collective-permute-start(bf16[1,256,4096]{2,1,0:T(8,128)(2,1)} %reshape.38), channel_id=1, source_target_pairs={{0,64},{64,128},{128,192},{192,256},{256,320},{320,384},{384,448},... | collective-permute-start | bytes 6291464 | tf_op jit(solution)/shard_map/ppermute | solution.py:19
Sparse Core Ops, SparseCore 0:
  10.7 94.1 all-gather.1
where the time goes:
time: 247 us; the launch traced here: 246 us
  waiting for transfers between devices  141 us (57%)
  local copies, waits for them, and re-layouts  44.8 us (18%)
  loops' own time  20.2 us (8%)
  matrix products  16.1 us (7%)
  between operations  13.5 us (5%)
  other arithmetic  7.2 us (3%)
  starting transfers between devices  3.26 us (1%)
    all_gather x1, waiting for transfers between devices, on_device(): complete = lax.all_gather(prefix_kv, 'tok', axis=1, tiled=True)  91.7 us
    ppermute x1, waiting for transfers between devices, from_behind(): lax.ppermute(x, axis, [(i, (i + by) % devices) for i in range(devices)])  48.2 us
    another operation x1, loops' own time, on_device(): results = lax.map(per_item, jnp.arange(QB_DEV * KV_HEADS))  20.2 us
    dot_general x8, matrix products, attend(): jnp.einsum('gqk,kd->qgd', weights, value_rows, preferred_element_type=jnp...  11.9 us
    dynamic_slice x16, local copies, waits for them, and re-layouts, per_item(): prefix_pairs[block_id, :, 1, head_id]  8.87 us
    unnamed x6, local copies, waits for them, and re-layouts  8.19 us
    dynamic_slice x8, local copies, waits for them, and re-layouts, per_item(): query_blocks[block_id, :, head_id]  7.81 us
  transfers between devices with their start and end apart: 2, of which 2 were waited for; matrix products, arithmetic and copies ran while one was open for 2% of the time, Pallas kernels for 0%

commit v1 on v0

v1 whole, which is shorter than its diff:
```python
import functools
import math

import jax
import jax.numpy as jnp
from jax import lax
from jax.experimental import pallas as pl
from jax.experimental.pallas import tpu as pltpu
from jax.sharding import PartitionSpec as P


Q_HEADS = 32
KV_HEADS = 4
GROUP = Q_HEADS // KV_HEADS
HEAD = 128
BLOCK = 128
PAGE = 64
DEPTH = 8
QB_DEV = 2
ROWS, CHIPS, CORES = 8, 4, 2
ROW_DEV = CHIPS * CORES
KEYS = DEPTH * PAGE + BLOCK

A_CHUNKS = ((0, 1),)
B_HEADS = (2, 3)


SMEM = functools.partial(pl.BlockSpec, memory_space=pltpu.SMEM)
VMEM = functools.partial(pl.BlockSpec, memory_space=pltpu.VMEM)


def next_section(x):
    n = lax.axis_size("section")
    return lax.ppermute(x, "section", [(i, (i + 1) % n) for i in range(n)])


def within_tok(x, chips=0, cores=0):
    pairs = []
    for row in range(ROWS):
        for chip in range(CHIPS):
            for core in range(CORES):
                there = (row * CHIPS + (chip + chips) % CHIPS) * CORES + (core + cores) % CORES
                pairs.append(((row * CHIPS + chip) * CORES + core, there))
    return lax.ppermute(x, "tok", pairs)


def across_rows(x):
    columns = [[row * ROW_DEV + at for row in range(ROWS)] for at in range(ROW_DEV)]
    return lax.all_to_all(x, "tok", 0, 0, axis_index_groups=columns, tiled=True)


def columns_of(heads):
    width = len(heads) * HEAD
    starts = (heads[0] * HEAD, (KV_HEADS + heads[0]) * HEAD)
    return [(i * width, (i + 1) * width, start, start + width) for i, start in enumerate(starts)]


def copies_kernel(columns, page, out):
    for to, to_end, start, end in columns:
        part = page[:, start:end]
        for i in range(out.shape[0]):
            out[i, :, to:to_end] = part


def stack_kernel(columns, *refs):
    out = refs[-1]
    for i, page in enumerate(refs[:-1]):
        for to, to_end, start, end in columns:
            out[i, :, to:to_end] = page[:, start:end]


def small_kernel(body, out_shape, *args):
    return pl.pallas_call(
        body,
        out_shape=out_shape,
        in_specs=[VMEM()] * len(args),
        out_specs=VMEM(),
        compiler_params=pltpu.CompilerParams(vmem_limit_bytes=4 << 20),
        cost_estimate=pl.CostEstimate(flops=0, transcendentals=0, bytes_accessed=1 << 20),
    )(*args)


def slot_of(served, block, level):
    pick = jnp.clip(served[block, level] - level * ROW_DEV, 0, ROW_DEV - 1)
    return pick // CORES, pick % CORES


def pick_for_rows_kernel(tok, served, mine, other, out):
    at = tok[0] % ROW_DEV
    level = tok[0] // ROW_DEV
    chip, core = at // CORES, at % CORES

    def one(i, carry):
        row, b = i // QB_DEV, i % QB_DEV
        owner_chip, owner_core = slot_of(served, (row * ROW_DEV + at) * QB_DEV + b, level)
        back = (chip - owner_chip + CHIPS) % CHIPS

        @pl.when(owner_core == core)
        def _():
            out[row, b] = mine[back]

        @pl.when(owner_core != core)
        def _():
            out[row, b] = other[back]

        return carry

    lax.fori_loop(0, ROWS * QB_DEV, one, 0)


def pick_for_rows(tok, served, mine, other):
    width = mine.shape[-1]
    return pl.pallas_call(
        pick_for_rows_kernel,
        out_shape=jax.ShapeDtypeStruct((ROWS, QB_DEV, PAGE, width), mine.dtype),
        in_specs=[SMEM(), SMEM(), VMEM(), VMEM()],
        out_specs=VMEM(),
        compiler_params=pltpu.CompilerParams(vmem_limit_bytes=16 << 20),
        cost_estimate=pl.CostEstimate(flops=0, transcendentals=0, bytes_accessed=4 << 20),
        name="pick_for_rows",
    )(tok, served, mine, other)


def pick_for_pair_kernel(tok, served, from0, from1, from2, from3, own, send):
    chip = tok[0] % ROW_DEV // CORES
    sources = (from0, from1, from2, from3)
    for b in range(QB_DEV):
        for level in range(DEPTH):
            for whose, out in ((tok[0], own), (tok[0] // CORES * CORES + 1 - tok[0] % CORES, send)):
                owner_chip, _ = slot_of(served, whose * QB_DEV + b, level)
                back = (chip - owner_chip + CHIPS) % CHIPS
                for d, source in enumerate(sources):

                    @pl.when(back == d)
                    def _(d=d, source=source, out=out):
                        out[b, level] = source[level]


def pick_for_pair(tok, served, sources):
    shape = jax.ShapeDtypeStruct((QB_DEV,) + sources[0].shape, sources[0].dtype)
    return pl.pallas_call(
        pick_for_pair_kernel,
        out_shape=(shape, shape),
        in_specs=[SMEM(), SMEM()] + [VMEM()] * CHIPS,
        out_specs=(VMEM(), VMEM()),
        compiler_params=pltpu.CompilerParams(vmem_limit_bytes=16 << 20),
        cost_estimate=pl.CostEstimate(flops=0, transcendentals=0, bytes_accessed=8 << 20),
        name="pick_for_pair",
    )(tok, served, *sources)


def attend(queries, own_keys, own_values, out, keys, values):
    keys[DEPTH * PAGE :, :] = own_keys[...]
    values[DEPTH * PAGE :, :HEAD] = own_values[...]
    values[DEPTH * PAGE :, HEAD:] = jnp.ones((BLOCK, HEAD), jnp.bfloat16)
    to_exp2 = math.log2(math.e) / math.sqrt(HEAD)
    row_index = lax.broadcasted_iota(jnp.int32, (BLOCK, BLOCK), 0)
    col_index = lax.broadcasted_iota(jnp.int32, (BLOCK, BLOCK), 1)
    causal = col_index <= row_index
    for g in range(GROUP):
        scores = lax.dot_general(
            queries[:, g * HEAD : (g + 1) * HEAD],
            keys[...],
            (((1,), (1,)), ((), ())),
            preferred_element_type=jnp.float32,
        )
        own = jnp.where(causal, scores[:, DEPTH * PAGE :], -jnp.inf)
        scores = jnp.concatenate([scores[:, : DEPTH * PAGE], own], axis=1)
        top = jnp.max(scores, axis=1, keepdims=True)
        weights = jnp.exp2((scores - top) * to_exp2).astype(jnp.bfloat16)
        mixed = jnp.dot(weights, values[...], preferred_element_type=jnp.float32)
        out[:, g * HEAD : (g + 1) * HEAD] = (mixed[:, :HEAD] / mixed[:, HEAD:]).astype(out.dtype)


def attend_kernel(y_first, tok, served, *refs):
    if y_first:
        own_k, own_v, pair_k, pair_v, queries, own_keys, own_values = refs[:7]
    else:
        page_k, page_v, queries, own_keys, own_values = refs[:5]
    out, keys, values = refs[-3:]
    block = tok[0] * QB_DEV + pl.program_id(1)
    core = tok[0] % CORES

    def put(level, key_rows, value_rows):
        rows = slice(level * PAGE, (level + 1) * PAGE)
        keys[rows, :] = key_rows
        values[rows, :HEAD] = value_rows
        values[rows, HEAD:] = jnp.ones((PAGE, HEAD), jnp.bfloat16)

    for level in range(DEPTH):
        live = served[block, level] >= 0
        if y_first:
            here = slot_of(served, block, level)[1] == core

            @pl.when(live & here)
            def _(level=level):
                put(level, own_k[0, level], own_v[0, level])

            @pl.when(live & jnp.logical_not(here))
            def _(level=level):
                put(level, pair_k[0, level], pair_v[0, level])

        else:

            @pl.when(live)
            def _(level=level):
                put(level, page_k[level, 0], page_v[level, 0])

        @pl.when(jnp.logical_not(live))
        def _(level=level):
            rows = slice(level * PAGE, (level + 1) * PAGE)
            keys[rows, :] = keys[:PAGE, :]
            values[rows, :] = jnp.zeros((PAGE, 2 * HEAD), jnp.bfloat16)

    attend(queries, own_keys, own_values, out, keys, values)


def attention(tok, served, pages, heads, queries, own_pairs, result):
    y_first = len(pages) == 2
    count, first = len(heads), heads[0]
    if y_first:
        page_block = (1, DEPTH, PAGE, HEAD)
        at = lambda part: pl.BlockSpec(page_block, lambda h, b: (b, 0, 0, part * count + h))
    else:
        page_block = (DEPTH, 1, PAGE, HEAD)
        at = lambda part: pl.BlockSpec(page_block, lambda h, b: (0, b, 0, part * count + h))
    wide = pl.BlockSpec((BLOCK, GROUP * HEAD), lambda h, b: (b, first + h))
    own = lambda part: pl.BlockSpec((BLOCK, HEAD), lambda h, b: (b, part * KV_HEADS + first + h))
    page_args, page_specs = [], []
    for page in pages:
        page_args += [page, page]
        page_specs += [at(0), at(1)]
    args = [tok, served] + page_args + [queries, own_pairs, own_pairs]
    specs = [SMEM(), SMEM()] + page_specs + [wide, own(0), own(1)]
    aliases = {}
    if result is not None:
        aliases = {len(args): 0}
        args.append(result)
        specs.append(pl.BlockSpec(memory_space=pl.ANY))
    items = count * QB_DEV * GROUP * BLOCK * KEYS
    return pl.pallas_call(
        functools.partial(attend_kernel, y_first),
        grid=(count, QB_DEV),
        out_shape=jax.ShapeDtypeStruct(queries.shape, queries.dtype),
        in_specs=specs,
        out_specs=wide,
        scratch_shapes=[pltpu.VMEM((KEYS, HEAD), jnp.bfloat16), pltpu.VMEM((KEYS, 2 * HEAD), jnp.bfloat16)],
        input_output_aliases=aliases,
        compiler_params=pltpu.CompilerParams(vmem_limit_bytes=24 << 20),
        cost_estimate=pl.CostEstimate(flops=items * 6 * HEAD, transcendentals=items, bytes_accessed=4 << 20),
        name="attend_b" if y_first else "attend_a",
    )(*args)


def on_device(queries, suffix_kv, prefix_kv, served):
    tok = lax.axis_index("tok").reshape(1)
    page = next_section(prefix_kv[0, 0])
    served = next_section(served[0])
    own_pairs = next_section(suffix_kv[0])
    queries = next_section(queries[0])

    def chip_copies(x):
        copies = [x]
        for d in range(1, CHIPS):
            copies.append(within_tok(x, chips=d))
        return copies

    width = 2 * len(B_HEADS) * HEAD
    level_b = small_kernel(
        functools.partial(copies_kernel, columns_of(B_HEADS)),
        jax.ShapeDtypeStruct((ROWS, PAGE, width), page.dtype),
        page,
    )
    level_b = across_rows(level_b)

    row_pages = chip_copies(page)
    a_heads = sum(A_CHUNKS, ())
    width = 2 * len(a_heads) * HEAD
    mine = small_kernel(
        functools.partial(stack_kernel, columns_of(a_heads)),
        jax.ShapeDtypeStruct((CHIPS, PAGE, width), page.dtype),
        *row_pages,
    )
    other = within_tok(mine, cores=1)

    result = None
    for heads in A_CHUNKS:
        sent = pick_for_rows(tok, served, mine, other)
        pages = across_rows(sent.reshape(ROWS, QB_DEV * PAGE, sent.shape[-1]))
        pages = pages.reshape(DEPTH, QB_DEV, PAGE, sent.shape[-1])
        result = attention(tok, served, (pages,), heads, queries, own_pairs, result)

    sources = chip_copies(level_b)
    own, send = pick_for_pair(tok, served, sources)
    pair = within_tok(send, cores=1)
    result = attention(tok, served, (own, pair), B_HEADS, queries, own_pairs, result)
    return result[None]


def solution(mesh):
    placed = (
        P("section", "tok", None),
        P("section", "tok", None),
        P("section", "tok", None, None),
        P("section", None, None),
    )
    return jax.shard_map(
        on_device, mesh=mesh, in_specs=placed, out_specs=P("section", "tok", None), check_vma=False
    )
```

time: 247 us -> 176 us (0.71)
  local copies, waits for them, and re-layouts: 44.8 us -> 0.11 us
  starting transfers between devices: 3.26 us -> 47.4 us
  waiting for transfers between devices: 141 us -> 101 us
  Pallas kernels: 0 us -> 26.3 us
  loops' own time: 20.2 us -> 0 us
  matrix products: 16.1 us -> 0 us
  between operations: 13.5 us -> 0.14 us
  other arithmetic: 7.2 us -> 0 us
    all_gather x1 -> x0, waiting for transfers between devices: 91.7 us -> none  [on_device(): complete = lax.all_gather(prefix_kv, 'tok', axis=1, tiled=True)]
    ppermute x1 -> x12, waiting for transfers between devices: 48.2 us -> 101 us  [the longest x4 72.6 us: next_section(): return lax.ppermute(x, 'section', [(i, (i + 1) % n) for i in range(n)])]
    ppermute x1 -> x12, starting transfers between devices: 3.26 us -> 33.8 us  [the longest x8 23.1 us: within_tok(): return lax.ppermute(x, 'tok', pairs)]
    pallas_call x0 -> x6, Pallas kernels: none -> 26.3 us  [the longest x2 18.3 us: attention(): pl.pallas_call(functools.partial(attend_kernel, y_first), grid=(count, QB...]
    dynamic_slice x56 -> x0, local copies, waits for them, and re-layouts: 22.8 us -> none  [the longest x16 8.87 us: per_item(): prefix_pairs[block_id, :, 1, head_id]]
    another operation x1 -> x0, loops' own time: 20.2 us -> none  [on_device(): results = lax.map(per_item, jnp.arange(QB_DEV * KV_HEADS))]
    dot_general x16 -> x0, matrix products: 16.1 us -> none  [the longest x8 11.9 us: attend(): jnp.einsum('gqk,kd->qgd', weights, value_rows, preferred_element_type=jnp...]
    all_to_all x0 -> x2, starting transfers between devices: none -> 13.6 us  [across_rows(): return lax.all_to_all(x, 'tok', 0, 0, axis_index_groups=columns, tiled=True)]
  transfers between devices with their start and end apart: 2 -> 14, of which waited for: 2 -> 8; matrix products, arithmetic and copies ran while one was open for 2% -> 0% of each run, Pallas kernels for 0% -> 9%
where the time goes in v1:
time: 176 us; the launch traced here: 175 us
  waiting for transfers between devices  101 us (57%)
  starting transfers between devices  47.4 us (27%)
  Pallas kernels  26.3 us (15%)
    ppermute x4, waiting for transfers between devices, next_section(): return lax.ppermute(x, 'section', [(i, (i + 1) % n) for i in range(n)])  72.6 us
    ppermute x8, waiting for transfers between devices, within_tok(): return lax.ppermute(x, 'tok', pairs)  28.8 us
    ppermute x8, starting transfers between devices, within_tok(): return lax.ppermute(x, 'tok', pairs)  23.1 us
    pallas_call x2, Pallas kernels, attention(): pl.pallas_call(functools.partial(attend_kernel, y_first), grid=(count, QB...  18.3 us
    all_to_all x2, starting transfers between devices, across_rows(): return lax.all_to_all(x, 'tok', 0, 0, axis_index_groups=columns, tiled=True)  13.6 us
    ppermute x4, starting transfers between devices, next_section(): return lax.ppermute(x, 'section', [(i, (i + 1) % n) for i in range(n)])  10.7 us
    pallas_call x1, Pallas kernels, pick_for_pair(): pl.pallas_call(pick_for_pair_kernel, out_shape=(shape, shape), in_specs=[...  3.86 us
  transfers between devices with their start and end apart: 14, of which 8 were waited for; matrix products, arithmetic and copies ran while one was open for 0% of the time, Pallas kernels for 9%

profile of v1, /device:TPU:1, one launch (start us, length us, event | category | flops | bytes accessed | tf_op | source)
XLA Modules:
  0.0 175.4 jit_solution(4141720524687891403)
XLA Ops:
  0.0 4.9 %collective-permute-start.1 = (bf16[64,1024]{1,0:T(8,128)(2,1)}, bf16[64,1024]{1,0:T(8,128)(2,1)S(1)}, u32[]{:S(2)}, u32[]{:S(2)}) collective-permute-start(bf16[64,1024]{1,0:T(8,128)(2,1)} %bitcast.10), channel_id=1, source_target_pairs={{0,64},{64,128},{128,192},{192,256},{256,320},{320,384},{384,448},... | collective-permute-start | bytes 393224 | tf_op jit(solution)/shard_map/ppermute | solution.py:34
  4.9 10.1 %collective-permute-done.1.page.refs_0_ = bf16[64,1024]{1,0:T(8,128)(2,1)S(1)} collective-permute-done((bf16[64,1024]{1,0:T(8,128)(2,1)}, bf16[64,1024]{1,0:T(8,128)(2,1)S(1)}, u32[]{:S(2)}, u32[]{:S(2)}) %collective-permute-start.1) | collective-permute-done | bytes 131104 | tf_op jit(solution)/shard_map/ppermute | solution.py:34
  15.0 0.8 shard_map.46
  15.9 6.8 %all-to-all-start = ((bf16[8,64,512]{2,1,0:T(8,128)(2,1)}), bf16[8,64,512]{2,1,0:T(8,128)(2,1)S(1)}, u32[]{:S(2)}, u32[]{:S(2)}) async-start(bf16[8,64,512]{2,1,0:T(8,128)(2,1)} %shard_map.46), calls=%async_computation | async-start | bytes 1048576 | tf_op jit(solution)/shard_map/all_to_all | solution.py:49
  22.7 4.4 %collective-permute-start.10 = (bf16[64,1024]{1,0:T(8,128)(2,1)S(1)}, bf16[64,1024]{1,0:T(8,128)(2,1)S(1)}, u32[]{:S(2)}, u32[]{:S(2)}) collective-permute-start(bf16[64,1024]{1,0:T(8,128)(2,1)S(1)} %collective-permute-done.1.page.refs_0_), channel_id=1, source_target_pairs={{0,6},{1,7},{2,0},{3,1},{4,2},{5,3},{6,4},{7,5},{8,14},{9,15},{10,... | collective-permute-start | bytes 393224 | tf_op jit(solution)/shard_map/ppermute | solution.py:44
  27.1 2.4 %collective-permute-start.9 = (bf16[64,1024]{1,0:T(8,128)(2,1)S(1)}, bf16[64,1024]{1,0:T(8,128)(2,1)S(1)}, u32[]{:S(2)}, u32[]{:S(2)}) collective-permute-start(bf16[64,1024]{1,0:T(8,128)(2,1)S(1)} %collective-permute-done.1.page.refs_0_), channel_id=1, source_target_pairs={{0,4},{1,5},{2,6},{3,7},{4,0},{5,1},{6,2},{7,3},{8,12},{9,13},{10,... | collective-permute-start | bytes 393224 | tf_op jit(solution)/shard_map/ppermute | solution.py:44
  29.5 2.5 %collective-permute-start.8 = (bf16[64,1024]{1,0:T(8,128)(2,1)S(1)}, bf16[64,1024]{1,0:T(8,128)(2,1)S(1)}, u32[]{:S(2)}, u32[]{:S(2)}) collective-permute-start(bf16[64,1024]{1,0:T(8,128)(2,1)S(1)} %collective-permute-done.1.page.refs_0_), channel_id=1, source_target_pairs={{0,2},{1,3},{2,4},{3,5},{4,6},{5,7},{6,0},{7,1},{8,10},{9,11},{10,... | collective-permute-start | bytes 393224 | tf_op jit(solution)/shard_map/ppermute | solution.py:44
  32.0 2.5 %collective-permute-done.9.refs_2_ = bf16[64,1024]{1,0:T(8,128)(2,1)S(1)} collective-permute-done((bf16[64,1024]{1,0:T(8,128)(2,1)S(1)}, bf16[64,1024]{1,0:T(8,128)(2,1)S(1)}, u32[]{:S(2)}, u32[]{:S(2)}) %collective-permute-start.9) | collective-permute-done | bytes 131104 | tf_op jit(solution)/shard_map/ppermute | solution.py:44
  34.6 3.7 %collective-permute-done.8.refs_1_ = bf16[64,1024]{1,0:T(8,128)(2,1)S(1)} collective-permute-done((bf16[64,1024]{1,0:T(8,128)(2,1)S(1)}, bf16[64,1024]{1,0:T(8,128)(2,1)S(1)}, u32[]{:S(2)}, u32[]{:S(2)}) %collective-permute-start.8) | collective-permute-done | bytes 131104 | tf_op jit(solution)/shard_map/ppermute | solution.py:44
  38.3 3.6 %collective-permute-start.11 = (bf16[4,64,512]{2,1,0:T(8,128)(2,1)S(1)}, bf16[4,64,512]{2,1,0:T(8,128)(2,1)S(1)}, u32[]{:S(2)}, u32[]{:S(2)}) collective-permute-start(bf16[4,64,512]{2,1,0:T(8,128)(2,1)S(1)} %shard_map.47.mine), channel_id=1, source_target_pairs={{0,1},{1,0},{2,3},{3,2},{4,5},{5,4},{6,7},{7,6},{8,9},{9,8},{10,11... | collective-permute-start | bytes 786440 | tf_op jit(solution)/shard_map/ppermute | solution.py:44
  41.9 1.9 %collective-permute-start.6 = (bf16[256,4096]{1,0:T(8,128)(2,1)}, bf16[256,4096]{1,0:T(8,128)(2,1)}, u32[]{:S(2)}, u32[]{:S(2)}) collective-permute-start(bf16[256,4096]{1,0:T(8,128)(2,1)} %bitcast.3), channel_id=1, source_target_pairs={{0,64},{64,128},{128,192},{192,256},{256,320},{320,384},{384,448},... | collective-permute-start | bytes 6291464 | tf_op jit(solution)/shard_map/ppermute | solution.py:34
  43.8 0.1 copy.6
  43.9 1.9 %collective-permute-start = (s32[128,8]{1,0:T(8,128)S(1)}, s32[128,8]{1,0:T(8,128)S(1)}, u32[]{:S(2)}, u32[]{:S(2)}) collective-permute-start(s32[128,8]{1,0:T(8,128)S(1)} %bitcast.8), channel_id=1, source_target_pairs={{0,64},{64,128},{128,192},{192,256},{256,320},{320,384},{384,448},... | collective-permute-start | bytes 12296 | tf_op jit(solution)/shard_map/ppermute | solution.py:34
  45.8 47.9 %collective-permute-done.served = s32[128,8]{1,0:T(8,128)S(1)} collective-permute-done((s32[128,8]{1,0:T(8,128)S(1)}, s32[128,8]{1,0:T(8,128)S(1)}, u32[]{:S(2)}, u32[]{:S(2)}) %collective-permute-start) | collective-permute-done | bytes 4128 | tf_op jit(solution)/shard_map/ppermute | solution.py:34
  93.8 3.3 %pick_for_rows.1 = bf16[8,2,64,512]{3,2,1,0:T(8,128)(2,1)} custom-call(s32[1]{0:T(128)} %bitcast.tok, s32[128,8]{1,0:T(8,128)S(1)} %collective-permute-done.served, bf16[4,64,512]{2,1,0:T(8,128)(2,1)S(1)} %shard_map.47.mine, bf16[4,64,512]{2,1,0:T(8,128)(2,1)S(1)} %collective-permute-done.11.other), custom_call_target="tpu_custom_call" | custom-call | bytes 4194304 | tf_op jit(solution)/shard_map/pick_for_rows/pallas_call | solution.py:113
  97.0 0.0 all-to-all-done.from0
  97.0 6.8 %all-to-all-start.1 = ((bf16[8,128,512]{2,1,0:T(8,128)(2,1)}), bf16[8,128,512]{2,1,0:T(8,128)(2,1)}, u32[]{:S(2)}, u32[]{:S(2)}) async-start(bf16[8,128,512]{2,1,0:T(8,128)(2,1)} %bitcast.5), calls=%async_computation.1 | async-start | bytes 2097152 | tf_op jit(solution)/shard_map/all_to_all | solution.py:49
  103.8 2.0 %collective-permute-start.4 = (bf16[8,64,512]{2,1,0:T(8,128)(2,1)S(1)}, bf16[8,64,512]{2,1,0:T(8,128)(2,1)S(1)}, u32[]{:S(2)}, u32[]{:S(2)}) collective-permute-start(bf16[8,64,512]{2,1,0:T(8,128)(2,1)S(1)} %all-to-all-done.from0), channel_id=1, source_target_pairs={{0,6},{1,7},{2,0},{3,1},{4,2},{5,3},{6,4},{7,5},{8,14},{9,15},{10,... | collective-permute-start | bytes 1572872 | tf_op jit(solution)/shard_map/ppermute | solution.py:44
  105.8 3.1 %collective-permute-start.3 = (bf16[8,64,512]{2,1,0:T(8,128)(2,1)S(1)}, bf16[8,64,512]{2,1,0:T(8,128)(2,1)S(1)}, u32[]{:S(2)}, u32[]{:S(2)}) collective-permute-start(bf16[8,64,512]{2,1,0:T(8,128)(2,1)S(1)} %all-to-all-done.from0), channel_id=1, source_target_pairs={{0,4},{1,5},{2,6},{3,7},{4,0},{5,1},{6,2},{7,3},{8,12},{9,13},{10,... | collective-permute-start | bytes 1572872 | tf_op jit(solution)/shard_map/ppermute | solution.py:44
  108.9 2.8 %collective-permute-start.2 = (bf16[8,64,512]{2,1,0:T(8,128)(2,1)S(1)}, bf16[8,64,512]{2,1,0:T(8,128)(2,1)S(1)}, u32[]{:S(2)}, u32[]{:S(2)}) collective-permute-start(bf16[8,64,512]{2,1,0:T(8,128)(2,1)S(1)} %all-to-all-done.from0), channel_id=1, source_target_pairs={{0,2},{1,3},{2,4},{3,5},{4,6},{5,7},{6,0},{7,1},{8,10},{9,11},{10,... | collective-permute-start | bytes 1572872 | tf_op jit(solution)/shard_map/ppermute | solution.py:44
  111.6 6.5 %collective-permute-done.4.from3 = bf16[8,64,512]{2,1,0:T(8,128)(2,1)S(1)} collective-permute-done((bf16[8,64,512]{2,1,0:T(8,128)(2,1)S(1)}, bf16[8,64,512]{2,1,0:T(8,128)(2,1)S(1)}, u32[]{:S(2)}, u32[]{:S(2)}) %collective-permute-start.4) | collective-permute-done | bytes 524320 | tf_op jit(solution)/shard_map/ppermute | solution.py:44
  118.1 3.3 %collective-permute-done.3.from2 = bf16[8,64,512]{2,1,0:T(8,128)(2,1)S(1)} collective-permute-done((bf16[8,64,512]{2,1,0:T(8,128)(2,1)S(1)}, bf16[8,64,512]{2,1,0:T(8,128)(2,1)S(1)}, u32[]{:S(2)}, u32[]{:S(2)}) %collective-permute-start.3) | collective-permute-done | bytes 524320 | tf_op jit(solution)/shard_map/ppermute | solution.py:44
  121.4 12.9 %collective-permute-done.2.from1 = bf16[8,64,512]{2,1,0:T(8,128)(2,1)S(1)} collective-permute-done((bf16[8,64,512]{2,1,0:T(8,128)(2,1)S(1)}, bf16[8,64,512]{2,1,0:T(8,128)(2,1)S(1)}, u32[]{:S(2)}, u32[]{:S(2)}) %collective-permute-start.2) | collective-permute-done | bytes 524320 | tf_op jit(solution)/shard_map/ppermute | solution.py:44
  134.3 3.9 %pick_for_pair.1 = (bf16[2,8,64,512]{3,2,1,0:T(8,128)(2,1)S(1)}, bf16[2,8,64,512]{3,2,1,0:T(8,128)(2,1)}) custom-call(s32[1]{0:T(128)} %bitcast.tok, s32[128,8]{1,0:T(8,128)S(1)} %collective-permute-done.served, bf16[8,64,512]{2,1,0:T(8,128)(2,1)S(1)} %all-to-all-done.from0, bf16[8,64,512]{2,1,0:T(8,128)(2,1)S(1)} %collective-permute-done.2.from1, ...), custom_call_target="tpu_custom_call" | custom-call | bytes 8388608 | tf_op jit(solution)/shard_map/pick_for_pair/pallas_call | solution.py:141
  138.1 2.4 %collective-permute-start.5 = (bf16[2,8,64,512]{3,2,1,0:T(8,128)(2,1)}, bf16[2,8,64,512]{3,2,1,0:T(8,128)(2,1)S(1)}, u32[]{:S(2)}, u32[]{:S(2)}) collective-permute-start(bf16[2,8,64,512]{3,2,1,0:T(8,128)(2,1)} %get-tuple-element.8), channel_id=1, source_target_pairs={{0,1},{1,0},{2,3},{3,2},{4,5},{5,4},{6,7},{7,6},{8,9},{9,8},{10,11... | collective-permute-start | bytes 3145736 | tf_op jit(solution)/shard_map/ppermute | solution.py:44
  140.5 1.9 %collective-permute-start.7 = (bf16[256,1024]{1,0:T(8,128)(2,1)S(1)}, bf16[256,1024]{1,0:T(8,128)(2,1)S(1)}, u32[]{:S(2)}, u32[]{:S(2)}) collective-permute-start(bf16[256,1024]{1,0:T(8,128)(2,1)S(1)} %bitcast.9), channel_id=1, source_target_pairs={{0,64},{64,128},{128,192},{192,256},{256,320},{320,384},{384,448},... | collective-permute-start | bytes 1572872 | tf_op jit(solution)/shard_map/ppermute | solution.py:34
  142.5 14.6 %collective-permute-done.7.refs_3_.refs_4_.refs_5_.refs_6_ = bf16[256,1024]{1,0:T(8,128)(2,1)S(1)} collective-permute-done((bf16[256,1024]{1,0:T(8,128)(2,1)S(1)}, bf16[256,1024]{1,0:T(8,128)(2,1)S(1)}, u32[]{:S(2)}, u32[]{:S(2)}) %collective-permute-start.7) | collective-permute-done | bytes 524320 | tf_op jit(solution)/shard_map/ppermute | solution.py:34
  157.1 0.0 collective-permute-done.6.refs_2_.refs_4_
  157.1 0.0 all-to-all-done.1
  157.1 8.8 %attend_a.1.refs_7_ = bf16[256,4096]{1,0:T(8,128)(2,1)} custom-call(s32[1]{0:T(128)} %bitcast.tok, s32[128,8]{1,0:T(8,128)S(1)} %collective-permute-done.served, bf16[8,2,64,512]{3,2,1,0:T(8,128)(2,1)} %bitcast.6.refs_0_.refs_1_, bf16[8,2,64,512]{3,2,1,0:T(8,128)(2,1)} %bitcast.6.refs_0_.refs_1_, bf16[256,4096]{1,0:T(8,128)(2,1)} %collective-permute-done.6.refs_2_.refs_4_, ...), custom_call_target="tpu_custom_call" | custom-call | flops 2013265920 | bytes 4194304 | tf_op jit(solution)/shard_map/attend_a/pallas_call | solution.py:241
  165.9 0.0 collective-permute-done.5.refs_2_.refs_3_
  165.9 9.5 %attend_b.1 = bf16[256,4096]{1,0:T(8,128)(2,1)} custom-call(s32[1]{0:T(128)} %bitcast.tok, s32[128,8]{1,0:T(8,128)S(1)} %collective-permute-done.served, bf16[2,8,64,512]{3,2,1,0:T(8,128)(2,1)S(1)} %get-tuple-element.7.refs_0_.refs_1_, bf16[2,8,64,512]{3,2,1,0:T(8,128)(2,1)S(1)} %get-tuple-element.7.refs_0_.refs_1_, ...), custom_call_target="tpu_custom_call", output_to_operand_aliasing={{}: (9, {})} | custom-call | flops 2013265920 | bytes 4194304 | tf_op jit(solution)/shard_map/attend_b/pallas_call | solution.py:241
  (7 shorter events, 0.0 us)
Async XLA Ops:
  0.0 43.8 %copy-start = (s32[1,128,8]{1,2,0:T(8,128)S(1)}, s32[1,128,8]{1,2,0:T(8,128)}, u32[]{:S(2)}) copy-start(s32[1,128,8]{1,2,0:T(8,128)} %param.7) | copy-start | bytes 12292
  0.0 15.0 %collective-permute-start.1 = (bf16[64,1024]{1,0:T(8,128)(2,1)}, bf16[64,1024]{1,0:T(8,128)(2,1)S(1)}, u32[]{:S(2)}, u32[]{:S(2)}) collective-permute-start(bf16[64,1024]{1,0:T(8,128)(2,1)} %bitcast.10), channel_id=1, source_target_pairs={{0,64},{64,128},{128,192},{192,256},{256,320},{320,384},{384,448},... | collective-permute-start | bytes 393224 | tf_op jit(solution)/shard_map/ppermute | solution.py:34
  15.9 81.2 %all-to-all-start = ((bf16[8,64,512]{2,1,0:T(8,128)(2,1)}), bf16[8,64,512]{2,1,0:T(8,128)(2,1)S(1)}, u32[]{:S(2)}, u32[]{:S(2)}) async-start(bf16[8,64,512]{2,1,0:T(8,128)(2,1)} %shard_map.46), calls=%async_computation | async-start | bytes 1048576 | tf_op jit(solution)/shard_map/all_to_all | solution.py:49
  22.7 9.3 %collective-permute-start.10 = (bf16[64,1024]{1,0:T(8,128)(2,1)S(1)}, bf16[64,1024]{1,0:T(8,128)(2,1)S(1)}, u32[]{:S(2)}, u32[]{:S(2)}) collective-permute-start(bf16[64,1024]{1,0:T(8,128)(2,1)S(1)} %collective-permute-done.1.page.refs_0_), channel_id=1, source_target_pairs={{0,6},{1,7},{2,0},{3,1},{4,2},{5,3},{6,4},{7,5},{8,14},{9,15},{10,... | collective-permute-start | bytes 393224 | tf_op jit(solution)/shard_map/ppermute | solution.py:44
  27.1 7.5 %collective-permute-start.9 = (bf16[64,1024]{1,0:T(8,128)(2,1)S(1)}, bf16[64,1024]{1,0:T(8,128)(2,1)S(1)}, u32[]{:S(2)}, u32[]{:S(2)}) collective-permute-start(bf16[64,1024]{1,0:T(8,128)(2,1)S(1)} %collective-permute-done.1.page.refs_0_), channel_id=1, source_target_pairs={{0,4},{1,5},{2,6},{3,7},{4,0},{5,1},{6,2},{7,3},{8,12},{9,13},{10,... | collective-permute-start | bytes 393224 | tf_op jit(solution)/shard_map/ppermute | solution.py:44
  29.5 8.7 %collective-permute-start.8 = (bf16[64,1024]{1,0:T(8,128)(2,1)S(1)}, bf16[64,1024]{1,0:T(8,128)(2,1)S(1)}, u32[]{:S(2)}, u32[]{:S(2)}) collective-permute-start(bf16[64,1024]{1,0:T(8,128)(2,1)S(1)} %collective-permute-done.1.page.refs_0_), channel_id=1, source_target_pairs={{0,2},{1,3},{2,4},{3,5},{4,6},{5,7},{6,0},{7,1},{8,10},{9,11},{10,... | collective-permute-start | bytes 393224 | tf_op jit(solution)/shard_map/ppermute | solution.py:44
  38.3 55.5 %collective-permute-start.11 = (bf16[4,64,512]{2,1,0:T(8,128)(2,1)S(1)}, bf16[4,64,512]{2,1,0:T(8,128)(2,1)S(1)}, u32[]{:S(2)}, u32[]{:S(2)}) collective-permute-start(bf16[4,64,512]{2,1,0:T(8,128)(2,1)S(1)} %shard_map.47.mine), channel_id=1, source_target_pairs={{0,1},{1,0},{2,3},{3,2},{4,5},{5,4},{6,7},{7,6},{8,9},{9,8},{10,11... | collective-permute-start | bytes 786440 | tf_op jit(solution)/shard_map/ppermute | solution.py:44
  41.9 115.2 %collective-permute-start.6 = (bf16[256,4096]{1,0:T(8,128)(2,1)}, bf16[256,4096]{1,0:T(8,128)(2,1)}, u32[]{:S(2)}, u32[]{:S(2)}) collective-permute-start(bf16[256,4096]{1,0:T(8,128)(2,1)} %bitcast.3), channel_id=1, source_target_pairs={{0,64},{64,128},{128,192},{192,256},{256,320},{320,384},{384,448},... | collective-permute-start | bytes 6291464 | tf_op jit(solution)/shard_map/ppermute | solution.py:34
  43.9 49.9 %collective-permute-start = (s32[128,8]{1,0:T(8,128)S(1)}, s32[128,8]{1,0:T(8,128)S(1)}, u32[]{:S(2)}, u32[]{:S(2)}) collective-permute-start(s32[128,8]{1,0:T(8,128)S(1)} %bitcast.8), channel_id=1, source_target_pairs={{0,64},{64,128},{128,192},{192,256},{256,320},{320,384},{384,448},... | collective-permute-start | bytes 12296 | tf_op jit(solution)/shard_map/ppermute | solution.py:34
  97.0 43.5 %copy-start.1 = (bf16[1,256,1024]{2,1,0:T(8,128)(2,1)S(1)}, bf16[1,256,1024]{2,1,0:T(8,128)(2,1)}, u32[]{:S(2)}) copy-start(bf16[1,256,1024]{2,1,0:T(8,128)(2,1)} %param.5) | copy-start | bytes 1572868
  97.0 60.1 %all-to-all-start.1 = ((bf16[8,128,512]{2,1,0:T(8,128)(2,1)}), bf16[8,128,512]{2,1,0:T(8,128)(2,1)}, u32[]{:S(2)}, u32[]{:S(2)}) async-start(bf16[8,128,512]{2,1,0:T(8,128)(2,1)} %bitcast.5), calls=%async_computation.1 | async-start | bytes 2097152 | tf_op jit(solution)/shard_map/all_to_all | solution.py:49
  103.8 14.3 %collective-permute-start.4 = (bf16[8,64,512]{2,1,0:T(8,128)(2,1)S(1)}, bf16[8,64,512]{2,1,0:T(8,128)(2,1)S(1)}, u32[]{:S(2)}, u32[]{:S(2)}) collective-permute-start(bf16[8,64,512]{2,1,0:T(8,128)(2,1)S(1)} %all-to-all-done.from0), channel_id=1, source_target_pairs={{0,6},{1,7},{2,0},{3,1},{4,2},{5,3},{6,4},{7,5},{8,14},{9,15},{10,... | collective-permute-start | bytes 1572872 | tf_op jit(solution)/shard_map/ppermute | solution.py:44
  105.8 15.6 %collective-permute-start.3 = (bf16[8,64,512]{2,1,0:T(8,128)(2,1)S(1)}, bf16[8,64,512]{2,1,0:T(8,128)(2,1)S(1)}, u32[]{:S(2)}, u32[]{:S(2)}) collective-permute-start(bf16[8,64,512]{2,1,0:T(8,128)(2,1)S(1)} %all-to-all-done.from0), channel_id=1, source_target_pairs={{0,4},{1,5},{2,6},{3,7},{4,0},{5,1},{6,2},{7,3},{8,12},{9,13},{10,... | collective-permute-start | bytes 1572872 | tf_op jit(solution)/shard_map/ppermute | solution.py:44
  108.9 25.4 %collective-permute-start.2 = (bf16[8,64,512]{2,1,0:T(8,128)(2,1)S(1)}, bf16[8,64,512]{2,1,0:T(8,128)(2,1)S(1)}, u32[]{:S(2)}, u32[]{:S(2)}) collective-permute-start(bf16[8,64,512]{2,1,0:T(8,128)(2,1)S(1)} %all-to-all-done.from0), channel_id=1, source_target_pairs={{0,2},{1,3},{2,4},{3,5},{4,6},{5,7},{6,0},{7,1},{8,10},{9,11},{10,... | collective-permute-start | bytes 1572872 | tf_op jit(solution)/shard_map/ppermute | solution.py:44
  138.1 27.8 %collective-permute-start.5 = (bf16[2,8,64,512]{3,2,1,0:T(8,128)(2,1)}, bf16[2,8,64,512]{3,2,1,0:T(8,128)(2,1)S(1)}, u32[]{:S(2)}, u32[]{:S(2)}) collective-permute-start(bf16[2,8,64,512]{3,2,1,0:T(8,128)(2,1)} %get-tuple-element.8), channel_id=1, source_target_pairs={{0,1},{1,0},{2,3},{3,2},{4,5},{5,4},{6,7},{7,6},{8,9},{9,8},{10,11... | collective-permute-start | bytes 3145736 | tf_op jit(solution)/shard_map/ppermute | solution.py:44
  140.5 16.6 %collective-permute-start.7 = (bf16[256,1024]{1,0:T(8,128)(2,1)S(1)}, bf16[256,1024]{1,0:T(8,128)(2,1)S(1)}, u32[]{:S(2)}, u32[]{:S(2)}) collective-permute-start(bf16[256,1024]{1,0:T(8,128)(2,1)S(1)} %bitcast.9), channel_id=1, source_target_pairs={{0,64},{64,128},{128,192},{192,256},{256,320},{320,384},{384,448},... | collective-permute-start | bytes 1572872 | tf_op jit(solution)/shard_map/ppermute | solution.py:34

commit v2 on v1

v2 whole, which is shorter than its diff:
```python
import functools
import math

import jax
import jax.numpy as jnp
from jax import lax
from jax.experimental import pallas as pl
from jax.experimental.pallas import tpu as pltpu
from jax.sharding import PartitionSpec as P


Q_HEADS = 32
KV_HEADS = 4
GROUP = Q_HEADS // KV_HEADS
HEAD = 128
BLOCK = 128
PAGE = 64
DEPTH = 8
QB_DEV = 2
ROWS, CHIPS, CORES = 8, 4, 2
ROW_DEV = CHIPS * CORES
KEYS = DEPTH * PAGE + BLOCK

A_HEADS = (0, 1)
B_HEADS = (2, 3)


SMEM = functools.partial(pl.BlockSpec, memory_space=pltpu.SMEM)
VMEM = functools.partial(pl.BlockSpec, memory_space=pltpu.VMEM)


def next_section(x):
    n = lax.axis_size("section")
    return lax.ppermute(x, "section", [(i, (i + 1) % n) for i in range(n)])


def within_tok(x, chips=0, cores=0):
    pairs = []
    for row in range(ROWS):
        for chip in range(CHIPS):
            for core in range(CORES):
                there = (row * CHIPS + (chip + chips) % CHIPS) * CORES + (core + cores) % CORES
                pairs.append(((row * CHIPS + chip) * CORES + core, there))
    return lax.ppermute(x, "tok", pairs)


def across_rows(x):
    columns = [[row * ROW_DEV + at for row in range(ROWS)] for at in range(ROW_DEV)]
    return lax.all_to_all(x, "tok", 0, 0, axis_index_groups=columns, tiled=True)


def within_row(x):
    rows = [[row * ROW_DEV + at for at in range(ROW_DEV)] for row in range(ROWS)]
    return lax.all_to_all(x, "tok", 0, 0, axis_index_groups=rows, tiled=True)


def columns_of(heads):
    width = len(heads) * HEAD
    starts = (heads[0] * HEAD, (KV_HEADS + heads[0]) * HEAD)
    return [(i * width, (i + 1) * width, start, start + width) for i, start in enumerate(starts)]


def copies_kernel(columns, page, out):
    for to, to_end, start, end in columns:
        part = page[:, start:end]
        for i in range(out.shape[0]):
            out[i, :, to:to_end] = part


def copies(page, heads, count):
    return pl.pallas_call(
        functools.partial(copies_kernel, columns_of(heads)),
        out_shape=jax.ShapeDtypeStruct((count, PAGE, 2 * len(heads) * HEAD), page.dtype),
        in_specs=[VMEM()],
        out_specs=VMEM(),
        compiler_params=pltpu.CompilerParams(vmem_limit_bytes=4 << 20),
        cost_estimate=pl.CostEstimate(flops=0, transcendentals=0, bytes_accessed=1 << 20),
        name="copies",
    )(page)


def slot_of(served, block, level):
    pick = jnp.clip(served[block, level] - level * ROW_DEV, 0, ROW_DEV - 1)
    return pick >> 1, pick & (CORES - 1)


def place_of(tok):
    return tok >> 3, (tok >> 1) & (CHIPS - 1), tok & (CORES - 1)


def pick_for_rows_kernel(tok, served, pages, out):
    level = tok[0] >> 3
    at = tok[0] & (ROW_DEV - 1)
    for row in range(ROWS):
        for b in range(QB_DEV):
            owner_chip, owner_core = slot_of(served, (row * ROW_DEV + at) * QB_DEV + b, level)
            out[row, b] = pages[owner_chip * CORES + owner_core]


def pick_for_rows(tok, served, pages):
    return pl.pallas_call(
        pick_for_rows_kernel,
        out_shape=jax.ShapeDtypeStruct((ROWS, QB_DEV) + pages.shape[1:], pages.dtype),
        in_specs=[SMEM(), SMEM(), VMEM()],
        out_specs=VMEM(),
        compiler_params=pltpu.CompilerParams(vmem_limit_bytes=16 << 20),
        cost_estimate=pl.CostEstimate(flops=0, transcendentals=0, bytes_accessed=4 << 20),
        name="pick_for_rows",
    )(tok, served, pages)


def pick_for_pair_kernel(tok, served, from0, from1, from2, from3, own, send):
    _, chip, _ = place_of(tok[0])
    for b in range(QB_DEV):
        for level in range(DEPTH):
            for whose, out in ((tok[0], own), (tok[0] ^ 1, send)):
                owner_chip, _ = slot_of(served, whose * QB_DEV + b, level)
                back = (chip - owner_chip) & (CHIPS - 1)
                even = lax.select_n(back == 2, from0[level], from2[level])
                odd = lax.select_n(back == 3, from1[level], from3[level])
                out[b, level] = lax.select_n((back & 1) == 1, even, odd)


def pick_for_pair(tok, served, sources):
    shape = jax.ShapeDtypeStruct((QB_DEV,) + sources[0].shape, sources[0].dtype)
    return pl.pallas_call(
        pick_for_pair_kernel,
        out_shape=(shape, shape),
        in_specs=[SMEM(), SMEM()] + [VMEM()] * CHIPS,
        out_specs=(VMEM(), VMEM()),
        compiler_params=pltpu.CompilerParams(vmem_limit_bytes=16 << 20),
        cost_estimate=pl.CostEstimate(flops=0, transcendentals=0, bytes_accessed=8 << 20),
        name="pick_for_pair",
    )(tok, served, *sources)


def attend(queries, own_keys, own_values, out, keys, values):
    keys[DEPTH * PAGE :, :] = own_keys[...]
    values[DEPTH * PAGE :, :HEAD] = own_values[...]
    values[DEPTH * PAGE :, HEAD:] = jnp.ones((BLOCK, HEAD), jnp.bfloat16)
    to_exp2 = math.log2(math.e) / math.sqrt(HEAD)
    row_index = lax.broadcasted_iota(jnp.int32, (BLOCK, BLOCK), 0)
    col_index = lax.broadcasted_iota(jnp.int32, (BLOCK, BLOCK), 1)
    causal = jnp.where(col_index <= row_index, 0.0, -jnp.inf)
    causal = jnp.concatenate([causal, causal], axis=0)

    def head(g):
        return slice(g * HEAD, (g + 1) * HEAD)

    def score(pair):
        rows = jnp.concatenate([queries[:, head(2 * pair)], queries[:, head(2 * pair + 1)]], axis=0)
        return lax.dot_general(
            rows, keys[...], (((1,), (1,)), ((), ())), preferred_element_type=jnp.float32
        )

    def weigh(scores):
        prefix = scores[:, : DEPTH * PAGE]
        own = scores[:, DEPTH * PAGE :] + causal
        top = jnp.maximum(
            jnp.max(prefix, axis=1, keepdims=True), jnp.max(own, axis=1, keepdims=True)
        )
        parts = [jnp.exp2((part - top) * to_exp2).astype(jnp.bfloat16) for part in (prefix, own)]
        return jnp.concatenate(parts, axis=1)

    def mix(pair, weights):
        mixed = jnp.dot(weights, values[...], preferred_element_type=jnp.float32)
        mixed = (mixed[:, :HEAD] / mixed[:, HEAD:]).astype(out.dtype)
        out[:, head(2 * pair)] = mixed[:BLOCK]
        out[:, head(2 * pair + 1)] = mixed[BLOCK:]

    pairs = GROUP // 2
    scores, weights = score(0), None
    for pair in range(pairs + 1):
        ahead = score(pair + 1) if pair + 1 < pairs else None
        now = weigh(scores) if pair < pairs else None
        if weights is not None:
            mix(pair - 1, weights)
        scores, weights = ahead, now


def attend_kernel(y_first, tok, served, *refs):
    if y_first:
        own_k, own_v, pair_k, pair_v, queries, own_keys, own_values = refs[:7]
    else:
        page_k, page_v, queries, own_keys, own_values = refs[:5]
    out, keys, values = refs[-3:]
    block = tok[0] * QB_DEV + pl.program_id(1)
    core = tok[0] & (CORES - 1)
    first = None
    for level in range(DEPTH):
        if y_first:
            here = slot_of(served, block, level)[1] == core
            key_rows = lax.select_n(here, pair_k[0, level], own_k[0, level])
            value_rows = lax.select_n(here, pair_v[0, level], own_v[0, level])
        else:
            key_rows, value_rows = page_k[level, 0], page_v[level, 0]
        live = served[block, level] >= 0
        first = key_rows if level == 0 else first
        rows = slice(level * PAGE, (level + 1) * PAGE)
        nothing = jnp.zeros((PAGE, HEAD), jnp.bfloat16)
        keys[rows, :] = lax.select_n(live, first, key_rows)
        values[rows, :HEAD] = lax.select_n(live, nothing, value_rows)
        values[rows, HEAD:] = lax.select_n(live, nothing, jnp.ones((PAGE, HEAD), jnp.bfloat16))
    attend(queries, own_keys, own_values, out, keys, values)


def attention(tok, served, pages, heads, queries, pairs, result_heads=None):
    y_first = len(pages) == 2
    queries, queries_at = queries
    pairs, key_at, value_at = pairs
    page_heads, page_at = pages[0].shape[-1] // (2 * HEAD), heads[0]
    count = len(heads)
    if y_first:
        page_block = (1, DEPTH, PAGE, HEAD)
        at = lambda part: pl.BlockSpec(page_block, lambda h, b: (b, 0, 0, part * page_heads + page_at + h))
    else:
        page_block = (DEPTH, 1, PAGE, HEAD)
        at = lambda part: pl.BlockSpec(page_block, lambda h, b: (0, b, 0, part * page_heads + page_at + h))
    block = (BLOCK, GROUP * HEAD)
    own = lambda start: pl.BlockSpec((BLOCK, HEAD), lambda h, b: (b, start + h))
    page_args, page_specs = [], []
    for page in pages:
        page_args += [page, page]
        page_specs += [at(0), at(1)]
    items = count * QB_DEV * GROUP * BLOCK * KEYS
    return pl.pallas_call(
        functools.partial(attend_kernel, y_first),
        grid=(count, QB_DEV),
        out_shape=jax.ShapeDtypeStruct(
            (queries.shape[0], (result_heads or count) * GROUP * HEAD), queries.dtype
        ),
        in_specs=[SMEM(), SMEM()]
        + page_specs
        + [pl.BlockSpec(block, lambda h, b: (b, queries_at + h)), own(key_at), own(value_at)],
        out_specs=pl.BlockSpec(block, lambda h, b: (b, h)),
        scratch_shapes=[
            pltpu.VMEM((KEYS, HEAD), jnp.bfloat16),
            pltpu.VMEM((KEYS, 2 * HEAD), jnp.bfloat16),
        ],
        compiler_params=pltpu.CompilerParams(vmem_limit_bytes=24 << 20),
        cost_estimate=pl.CostEstimate(flops=items * 6 * HEAD, transcendentals=items, bytes_accessed=4 << 20),
        name="attend_b" if y_first else "attend_a",
    )(tok, served, *page_args, queries, pairs, pairs)


def on_device(queries, suffix_kv, prefix_kv, served):
    tok = lax.axis_index("tok").reshape(1)
    queries, suffix_kv, page, served = queries[0], suffix_kv[0], prefix_kv[0, 0], served[0]

    level_b = copies(page, B_HEADS, ROWS)
    level_b = across_rows(level_b)

    page_in = next_section(page)
    served_in = next_section(served)
    queries_in = next_section(queries[:, : len(A_HEADS) * GROUP * HEAD])
    pairs_in = jnp.concatenate(
        [suffix_kv[:, to_start:to_end] for _, _, to_start, to_end in columns_of(A_HEADS)], axis=1
    )
    pairs_in = next_section(pairs_in)

    row_pages = copies(page_in, A_HEADS, ROW_DEV)
    row_pages = within_row(row_pages)
    sent = pick_for_rows(tok, served_in, row_pages)
    pages = across_rows(sent.reshape(ROWS, QB_DEV * PAGE, -1))
    pages = pages.reshape(DEPTH, QB_DEV, PAGE, -1)

    sources = [level_b]
    for d in range(1, CHIPS):
        sources.append(within_tok(level_b, chips=d))
    own, send = pick_for_pair(tok, served, sources)
    pair = within_tok(send, cores=1)
    arrived = []
    for i, h in enumerate(B_HEADS):
        mixed = attention(
            tok, served, (own, pair), (i,), (queries, h), (suffix_kv, h, KV_HEADS + h)
        )
        arrived.append(next_section(mixed))

    result = attention(
        tok, served_in, (pages,), A_HEADS, (queries_in, 0), (pairs_in, 0, len(A_HEADS)), KV_HEADS
    )
    for h, mixed in zip(B_HEADS, arrived):
        result = lax.dynamic_update_slice(result, mixed, (0, h * GROUP * HEAD))
    return result[None]


def solution(mesh):
    placed = (
        P("section", "tok", None),
        P("section", "tok", None),
        P("section", "tok", None, None),
        P("section", None, None),
    )
    return jax.shard_map(
        on_device, mesh=mesh, in_specs=placed, out_specs=P("section", "tok", None), check_vma=False
    )
```

time: 176 us -> 135 us (0.77)
  waiting for transfers between devices: 101 us -> 47.8 us
  starting transfers between devices: 47.4 us -> 56.8 us
  local copies, waits for them, and re-layouts: 0.11 us -> 7.04 us
  Pallas kernels: 26.3 us -> 22.2 us
    ppermute x4 -> x6, waiting for transfers between devices: 72.6 us -> 43.7 us  [next_section(): return lax.ppermute(x, 'section', [(i, (i + 1) % n) for i in range(n)])]
    ppermute x8 -> x4, waiting for transfers between devices: 28.8 us -> 3.7 us  [within_tok(): return lax.ppermute(x, 'tok', pairs)]
    ppermute x4 -> x6, starting transfers between devices: 10.7 us -> 25.2 us  [next_section(): return lax.ppermute(x, 'section', [(i, (i + 1) % n) for i in range(n)])]
    ppermute x8 -> x4, starting transfers between devices: 23.1 us -> 11.8 us  [within_tok(): return lax.ppermute(x, 'tok', pairs)]
    all_to_all x0 -> x1, starting transfers between devices: none -> 7.8 us  [within_row(): return lax.all_to_all(x, 'tok', 0, 0, axis_index_groups=rows, tiled=True)]
    dynamic_update_slice x0 -> x2, local copies, waits for them, and re-layouts: none -> 3.74 us  [on_device(): result = lax.dynamic_update_slice(result, mixed, (0, h * GROUP * HEAD))]
    unnamed x5 -> x13, local copies, waits for them, and re-layouts: 0.11 us -> 3.21 us
    pallas_call x2 -> x3, Pallas kernels: 18.3 us -> 15.9 us  [attention(): pl.pallas_call(functools.partial(attend_kernel, y_first), grid=(count, QB...]
  transfers between devices with their start and end apart: 14 -> 13, of which waited for: 8 -> 5; matrix products, arithmetic and copies ran while one was open for 0% -> 2% of each run, Pallas kernels for 9% -> 16%
where the time goes in v2:
time: 135 us; the launch traced here: 134 us
  starting transfers between devices  56.8 us (42%)
  waiting for transfers between devices  47.8 us (35%)
  Pallas kernels  22.2 us (16%)
  local copies, waits for them, and re-layouts  7.04 us (5%)
    ppermute x6, waiting for transfers between devices, next_section(): return lax.ppermute(x, 'section', [(i, (i + 1) % n) for i in range(n)])  43.7 us
    ppermute x6, starting transfers between devices, next_section(): return lax.ppermute(x, 'section', [(i, (i + 1) % n) for i in range(n)])  25.2 us
    pallas_call x3, Pallas kernels, attention(): pl.pallas_call(functools.partial(attend_kernel, y_first), grid=(count, QB...  15.9 us
    all_to_all x2, starting transfers between devices, across_rows(): return lax.all_to_all(x, 'tok', 0, 0, axis_index_groups=columns, tiled=True)  12 us
    ppermute x4, starting transfers between devices, within_tok(): return lax.ppermute(x, 'tok', pairs)  11.8 us
    all_to_all x1, starting transfers between devices, within_row(): return lax.all_to_all(x, 'tok', 0, 0, axis_index_groups=rows, tiled=True)  7.8 us
    dynamic_update_slice x2, local copies, waits for them, and re-layouts, on_device(): result = lax.dynamic_update_slice(result, mixed, (0, h * GROUP * HEAD))  3.74 us
    ppermute x4, waiting for transfers between devices, within_tok(): return lax.ppermute(x, 'tok', pairs)  3.7 us
  transfers between devices with their start and end apart: 13, of which 5 were waited for; matrix products, arithmetic and copies ran while one was open for 2% of the time, Pallas kernels for 16%

profile of v2, /device:TPU:1, one launch (start us, length us, event | category | flops | bytes accessed | tf_op | source)
XLA Modules:
  0.0 134.1 jit_solution(13297589588872183047)
XLA Ops:
  0.0 0.9 copy-done.2
  0.9 0.8 copies.3
  1.8 7.6 %all-to-all-start.2 = ((bf16[8,64,512]{2,1,0:T(8,128)(2,1)}), bf16[8,64,512]{2,1,0:T(8,128)(2,1)S(1)}, u32[]{:S(2)}, u32[]{:S(2)}) async-start(bf16[8,64,512]{2,1,0:T(8,128)(2,1)} %copies.3), calls=%async_computation.2 | async-start | bytes 1048576 | tf_op jit(solution)/shard_map/all_to_all | solution.py:49
  9.4 4.0 %collective-permute-start.1 = (bf16[64,1024]{1,0:T(8,128)(2,1)}, bf16[64,1024]{1,0:T(8,128)(2,1)S(1)}, u32[]{:S(2)}, u32[]{:S(2)}) collective-permute-start(bf16[64,1024]{1,0:T(8,128)(2,1)} %bitcast.24), channel_id=1, source_target_pairs={{0,64},{64,128},{128,192},{192,256},{256,320},{320,384},{384,448},... | collective-permute-start | bytes 393224 | tf_op jit(solution)/shard_map/ppermute | solution.py:34
  13.4 9.8 %collective-permute-done.1.page = bf16[64,1024]{1,0:T(8,128)(2,1)S(1)} collective-permute-done((bf16[64,1024]{1,0:T(8,128)(2,1)}, bf16[64,1024]{1,0:T(8,128)(2,1)S(1)}, u32[]{:S(2)}, u32[]{:S(2)}) %collective-permute-start.1) | collective-permute-done | bytes 131104 | tf_op jit(solution)/shard_map/ppermute | solution.py:34
  23.2 0.8 copies.2
  24.0 0.3 all-to-all-done.2.from0
  24.3 7.8 %all-to-all-start = ((bf16[8,64,512]{2,1,0:T(8,128)(2,1)}), bf16[8,64,512]{2,1,0:T(8,128)(2,1)S(1)}, u32[]{:S(2)}, u32[]{:S(2)}) async-start(bf16[8,64,512]{2,1,0:T(8,128)(2,1)} %copies.2), calls=%async_computation | async-start | bytes 1048576 | tf_op jit(solution)/shard_map/all_to_all | solution.py:54
  32.1 4.5 %collective-permute-start.6 = (bf16[8,64,512]{2,1,0:T(8,128)(2,1)S(1)}, bf16[8,64,512]{2,1,0:T(8,128)(2,1)S(1)}, u32[]{:S(2)}, u32[]{:S(2)}) collective-permute-start(bf16[8,64,512]{2,1,0:T(8,128)(2,1)S(1)} %all-to-all-done.2.from0), channel_id=1, source_target_pairs={{0,6},{1,7},{2,0},{3,1},{4,2},{5,3},{6,4},{7,5},{8,14},{9,15},{10,... | collective-permute-start | bytes 1572872 | tf_op jit(solution)/shard_map/ppermute | solution.py:44
  36.6 2.5 %collective-permute-start.5 = (bf16[8,64,512]{2,1,0:T(8,128)(2,1)S(1)}, bf16[8,64,512]{2,1,0:T(8,128)(2,1)}, u32[]{:S(2)}, u32[]{:S(2)}) collective-permute-start(bf16[8,64,512]{2,1,0:T(8,128)(2,1)S(1)} %all-to-all-done.2.from0), channel_id=1, source_target_pairs={{0,4},{1,5},{2,6},{3,7},{4,0},{5,1},{6,2},{7,3},{8,12},{9,13},{10,... | collective-permute-start | bytes 1572872 | tf_op jit(solution)/shard_map/ppermute | solution.py:44
  39.1 2.5 %collective-permute-start.4 = (bf16[8,64,512]{2,1,0:T(8,128)(2,1)S(1)}, bf16[8,64,512]{2,1,0:T(8,128)(2,1)}, u32[]{:S(2)}, u32[]{:S(2)}) collective-permute-start(bf16[8,64,512]{2,1,0:T(8,128)(2,1)S(1)} %all-to-all-done.2.from0), channel_id=1, source_target_pairs={{0,2},{1,3},{2,4},{3,5},{4,6},{5,7},{6,0},{7,1},{8,10},{9,11},{10,... | collective-permute-start | bytes 1572872 | tf_op jit(solution)/shard_map/ppermute | solution.py:44
  41.6 0.1 copy.5
  41.7 4.0 %collective-permute-start = (s32[128,8]{1,0:T(8,128)S(1)}, s32[128,8]{1,0:T(8,128)S(1)}, u32[]{:S(2)}, u32[]{:S(2)}) collective-permute-start(s32[128,8]{1,0:T(8,128)S(1)} %bitcast.20), channel_id=1, source_target_pairs={{0,64},{64,128},{128,192},{192,256},{256,320},{320,384},{384,448},... | collective-permute-start | bytes 12296 | tf_op jit(solution)/shard_map/ppermute | solution.py:34
  45.7 8.7 %collective-permute-done.served = s32[128,8]{1,0:T(8,128)S(1)} collective-permute-done((s32[128,8]{1,0:T(8,128)S(1)}, s32[128,8]{1,0:T(8,128)S(1)}, u32[]{:S(2)}, u32[]{:S(2)}) %collective-permute-start) | collective-permute-done | bytes 4128 | tf_op jit(solution)/shard_map/ppermute | solution.py:34
  54.4 2.7 %pick_for_rows.1 = bf16[8,2,64,512]{3,2,1,0:T(8,128)(2,1)} custom-call(s32[1]{0:T(128)} %bitcast.tok, s32[128,8]{1,0:T(8,128)S(1)} %collective-permute-done.served, bf16[8,64,512]{2,1,0:T(8,128)(2,1)S(1)} %all-to-all-done.pages), custom_call_target="tpu_custom_call" | custom-call | bytes 4194304 | tf_op jit(solution)/shard_map/pick_for_rows/pallas_call | solution.py:101
  57.1 4.4 %all-to-all-start.1 = ((bf16[8,128,512]{2,1,0:T(8,128)(2,1)}), bf16[8,128,512]{2,1,0:T(8,128)(2,1)}, u32[]{:S(2)}, u32[]{:S(2)}) async-start(bf16[8,128,512]{2,1,0:T(8,128)(2,1)} %bitcast.3), calls=%async_computation.1 | async-start | bytes 2097152 | tf_op jit(solution)/shard_map/all_to_all | solution.py:49
  61.5 3.7 %collective-permute-done.4.from1 = bf16[8,64,512]{2,1,0:T(8,128)(2,1)} collective-permute-done((bf16[8,64,512]{2,1,0:T(8,128)(2,1)S(1)}, bf16[8,64,512]{2,1,0:T(8,128)(2,1)}, u32[]{:S(2)}, u32[]{:S(2)}) %collective-permute-start.4) | collective-permute-done | bytes 524320 | tf_op jit(solution)/shard_map/ppermute | solution.py:44
  65.2 1.9 %pick_for_pair.1 = (bf16[2,8,64,512]{3,2,1,0:T(8,128)(2,1)S(1)}, bf16[2,8,64,512]{3,2,1,0:T(8,128)(2,1)S(1)}) custom-call(s32[1]{0:T(128)} %bitcast.tok, s32[128,8]{1,0:T(8,128)S(1)} %bitcast.21, bf16[8,64,512]{2,1,0:T(8,128)(2,1)S(1)} %all-to-all-done.2.from0, bf16[8,64,512]{2,1,0:T(8,128)(2,1)} %collective-permute-done.4.from1, ...), custom_call_target="tpu_custom_call" | custom-call | bytes 8388608 | tf_op jit(solution)/shard_map/pick_for_pair/pallas_call | solution.py:126
  67.1 2.4 %collective-permute-start.7 = (bf16[2,8,64,512]{3,2,1,0:T(8,128)(2,1)S(1)}, bf16[2,8,64,512]{3,2,1,0:T(8,128)(2,1)S(1)}, u32[]{:S(2)}, u32[]{:S(2)}) collective-permute-start(bf16[2,8,64,512]{3,2,1,0:T(8,128)(2,1)S(1)} %get-tuple-element.8), channel_id=1, source_target_pairs={{0,1},{1,0},{2,3},{3,2},{4,5},{5,4},{6,7},{7,6},{8,9},{9,8},{10,11... | collective-permute-start | bytes 3145736 | tf_op jit(solution)/shard_map/ppermute | solution.py:44
  69.5 0.1 slice.12
  69.6 4.0 %collective-permute-start.2 = (bf16[256,2048]{1,0:T(8,128)(2,1)S(1)}, bf16[256,2048]{1,0:T(8,128)(2,1)S(1)}, u32[]{:S(2)}, u32[]{:S(2)}) collective-permute-start(bf16[256,2048]{1,0:T(8,128)(2,1)S(1)} %slice.12), channel_id=1, source_target_pairs={{0,64},{64,128},{128,192},{192,256},{256,320},{320,384},{384,448},... | collective-permute-start | bytes 3145736 | tf_op jit(solution)/shard_map/ppermute | solution.py:34
  73.7 4.2 %attend_b.2 = bf16[256,1024]{1,0:T(8,128)(2,1)S(1)} custom-call(s32[1]{0:T(128)} %bitcast.tok, s32[128,8]{1,0:T(8,128)S(1)} %bitcast.22, bf16[2,8,64,512]{3,2,1,0:T(8,128)(2,1)S(1)} %get-tuple-element.7.refs_0_.refs_1_, bf16[2,8,64,512]{3,2,1,0:T(8,128)(2,1)S(1)} %get-tuple-element.7.refs_0_.refs_1_, ...), custom_call_target="tpu_custom_call" | custom-call | flops 1006632960 | bytes 4194304 | tf_op jit(solution)/shard_map/attend_b/pallas_call | solution.py:226
  77.9 4.0 %collective-permute-start.8 = (bf16[256,1024]{1,0:T(8,128)(2,1)S(1)}, bf16[256,1024]{1,0:T(8,128)(2,1)}, u32[]{:S(2)}, u32[]{:S(2)}) collective-permute-start(bf16[256,1024]{1,0:T(8,128)(2,1)S(1)} %attend_b.2), channel_id=1, source_target_pairs={{0,64},{64,128},{128,192},{192,256},{256,320},{320,384},{384,448},... | collective-permute-start | bytes 1572872 | tf_op jit(solution)/shard_map/ppermute | solution.py:34
  81.9 4.0 %collective-permute-start.3 = (bf16[256,512]{1,0:T(8,128)(2,1)S(1)}, bf16[256,512]{1,0:T(8,128)(2,1)S(1)}, u32[]{:S(2)}, u32[]{:S(2)}) collective-permute-start(bf16[256,512]{1,0:T(8,128)(2,1)S(1)} %pad_maximum_fusion), channel_id=1, source_target_pairs={{0,64},{64,128},{128,192},{192,256},{256,320},{320,384},{384,448},... | collective-permute-start | bytes 786440 | tf_op jit(solution)/shard_map/ppermute | solution.py:34
  85.9 4.2 %attend_b.3 = bf16[256,1024]{1,0:T(8,128)(2,1)S(1)} custom-call(s32[1]{0:T(128)} %bitcast.tok, s32[128,8]{1,0:T(8,128)S(1)} %bitcast.23, bf16[2,8,64,512]{3,2,1,0:T(8,128)(2,1)S(1)} %get-tuple-element.7.refs_0_.refs_1_, bf16[2,8,64,512]{3,2,1,0:T(8,128)(2,1)S(1)} %get-tuple-element.7.refs_0_.refs_1_, ...), custom_call_target="tpu_custom_call" | custom-call | flops 1006632960 | bytes 4194304 | tf_op jit(solution)/shard_map/attend_b/pallas_call | solution.py:226
  90.2 5.2 %collective-permute-start.9 = (bf16[256,1024]{1,0:T(8,128)(2,1)S(1)}, bf16[256,1024]{1,0:T(8,128)(2,1)}, u32[]{:S(2)}, u32[]{:S(2)}) collective-permute-start(bf16[256,1024]{1,0:T(8,128)(2,1)S(1)} %attend_b.3), channel_id=1, source_target_pairs={{0,64},{64,128},{128,192},{192,256},{256,320},{320,384},{384,448},... | collective-permute-start | bytes 1572872 | tf_op jit(solution)/shard_map/ppermute | solution.py:34
  95.4 25.2 %collective-permute-done.3.refs_3_.refs_4_ = bf16[256,512]{1,0:T(8,128)(2,1)S(1)} collective-permute-done((bf16[256,512]{1,0:T(8,128)(2,1)S(1)}, bf16[256,512]{1,0:T(8,128)(2,1)S(1)}, u32[]{:S(2)}, u32[]{:S(2)}) %collective-permute-start.3) | collective-permute-done | bytes 262176 | tf_op jit(solution)/shard_map/ppermute | solution.py:34
  120.6 1.0 copy-done.3
  121.6 1.2 copy-done.4
  122.8 7.5 %attend_a.1 = bf16[256,4096]{1,0:T(8,128)(2,1)} custom-call(s32[1]{0:T(128)} %bitcast.tok, s32[128,8]{1,0:T(8,128)S(1)} %collective-permute-done.served, bf16[8,2,64,512]{3,2,1,0:T(8,128)(2,1)} %bitcast.4.refs_0_.refs_1_, bf16[8,2,64,512]{3,2,1,0:T(8,128)(2,1)} %bitcast.4.refs_0_.refs_1_, bf16[256,2048]{1,0:T(8,128)(2,1)S(1)} %copy-done.4, ...), custom_call_target="tpu_custom_call" | custom-call | flops 2013265920 | bytes 4194304 | tf_op jit(solution)/shard_map/attend_a/pallas_call | solution.py:226
  130.3 1.9 %bitcast_dynamic-update-slice_fusion.1 = bf16[1,256,4096]{2,1,0:T(8,128)(2,1)} fusion(bf16[1,256,4096]{2,1,0:T(8,128)(2,1)} %bitcast.26, bf16[256,1024]{1,0:T(8,128)(2,1)} %collective-permute-done.8), kind=kLoop, calls=%fused_computation.1 | loop fusion | bytes 1048576 | tf_op jit(solution)/shard_map/dynamic_update_slice | solution.py:283
  132.2 1.9 %bitcast_dynamic-update-slice_fusion = bf16[1,256,4096]{2,1,0:T(8,128)(2,1)} fusion(bf16[1,256,4096]{2,1,0:T(8,128)(2,1)} %bitcast_dynamic-update-slice_fusion.1, bf16[256,1024]{1,0:T(8,128)(2,1)} %collective-permute-done.9), kind=kLoop, calls=%fused_computation | loop fusion | bytes 1048576 | tf_op jit(solution)/shard_map/dynamic_update_slice | solution.py:283
  (19 shorter events, 0.1 us)
Async XLA Ops:
  0.0 0.9 copy-start.2
  0.9 40.7 %copy-start.5 = (s32[1,128,8]{1,2,0:T(8,128)S(1)}, s32[1,128,8]{1,2,0:T(8,128)}, u32[]{:S(2)}) copy-start(s32[1,128,8]{1,2,0:T(8,128)} %param.7) | copy-start | bytes 12292
  1.8 22.6 %all-to-all-start.2 = ((bf16[8,64,512]{2,1,0:T(8,128)(2,1)}), bf16[8,64,512]{2,1,0:T(8,128)(2,1)S(1)}, u32[]{:S(2)}, u32[]{:S(2)}) async-start(bf16[8,64,512]{2,1,0:T(8,128)(2,1)} %copies.3), calls=%async_computation.2 | async-start | bytes 1048576 | tf_op jit(solution)/shard_map/all_to_all | solution.py:49
  9.4 13.8 %collective-permute-start.1 = (bf16[64,1024]{1,0:T(8,128)(2,1)}, bf16[64,1024]{1,0:T(8,128)(2,1)S(1)}, u32[]{:S(2)}, u32[]{:S(2)}) collective-permute-start(bf16[64,1024]{1,0:T(8,128)(2,1)} %bitcast.24), channel_id=1, source_target_pairs={{0,64},{64,128},{128,192},{192,256},{256,320},{320,384},{384,448},... | collective-permute-start | bytes 393224 | tf_op jit(solution)/shard_map/ppermute | solution.py:34
  24.3 30.1 %all-to-all-start = ((bf16[8,64,512]{2,1,0:T(8,128)(2,1)}), bf16[8,64,512]{2,1,0:T(8,128)(2,1)S(1)}, u32[]{:S(2)}, u32[]{:S(2)}) async-start(bf16[8,64,512]{2,1,0:T(8,128)(2,1)} %copies.2), calls=%async_computation | async-start | bytes 1048576 | tf_op jit(solution)/shard_map/all_to_all | solution.py:54
  32.1 29.3 %collective-permute-start.6 = (bf16[8,64,512]{2,1,0:T(8,128)(2,1)S(1)}, bf16[8,64,512]{2,1,0:T(8,128)(2,1)S(1)}, u32[]{:S(2)}, u32[]{:S(2)}) collective-permute-start(bf16[8,64,512]{2,1,0:T(8,128)(2,1)S(1)} %all-to-all-done.2.from0), channel_id=1, source_target_pairs={{0,6},{1,7},{2,0},{3,1},{4,2},{5,3},{6,4},{7,5},{8,14},{9,15},{10,... | collective-permute-start | bytes 1572872 | tf_op jit(solution)/shard_map/ppermute | solution.py:44
  36.6 24.9 %collective-permute-start.5 = (bf16[8,64,512]{2,1,0:T(8,128)(2,1)S(1)}, bf16[8,64,512]{2,1,0:T(8,128)(2,1)}, u32[]{:S(2)}, u32[]{:S(2)}) collective-permute-start(bf16[8,64,512]{2,1,0:T(8,128)(2,1)S(1)} %all-to-all-done.2.from0), channel_id=1, source_target_pairs={{0,4},{1,5},{2,6},{3,7},{4,0},{5,1},{6,2},{7,3},{8,12},{9,13},{10,... | collective-permute-start | bytes 1572872 | tf_op jit(solution)/shard_map/ppermute | solution.py:44
  39.1 26.1 %collective-permute-start.4 = (bf16[8,64,512]{2,1,0:T(8,128)(2,1)S(1)}, bf16[8,64,512]{2,1,0:T(8,128)(2,1)}, u32[]{:S(2)}, u32[]{:S(2)}) collective-permute-start(bf16[8,64,512]{2,1,0:T(8,128)(2,1)S(1)} %all-to-all-done.2.from0), channel_id=1, source_target_pairs={{0,2},{1,3},{2,4},{3,5},{4,6},{5,7},{6,0},{7,1},{8,10},{9,11},{10,... | collective-permute-start | bytes 1572872 | tf_op jit(solution)/shard_map/ppermute | solution.py:44
  41.7 12.7 %collective-permute-start = (s32[128,8]{1,0:T(8,128)S(1)}, s32[128,8]{1,0:T(8,128)S(1)}, u32[]{:S(2)}, u32[]{:S(2)}) collective-permute-start(s32[128,8]{1,0:T(8,128)S(1)} %bitcast.20), channel_id=1, source_target_pairs={{0,64},{64,128},{128,192},{192,256},{256,320},{320,384},{384,448},... | collective-permute-start | bytes 12296 | tf_op jit(solution)/shard_map/ppermute | solution.py:34
  57.1 12.4 %copy-start = (bf16[1,256,4096]{2,1,0:T(8,128)(2,1)S(1)}, bf16[1,256,4096]{2,1,0:T(8,128)(2,1)}, u32[]{:S(2)}) copy-start(bf16[1,256,4096]{2,1,0:T(8,128)(2,1)} %param.4) | copy-start | bytes 6291460
  57.1 64.5 %all-to-all-start.1 = ((bf16[8,128,512]{2,1,0:T(8,128)(2,1)}), bf16[8,128,512]{2,1,0:T(8,128)(2,1)}, u32[]{:S(2)}, u32[]{:S(2)}) async-start(bf16[8,128,512]{2,1,0:T(8,128)(2,1)} %bitcast.3), calls=%async_computation.1 | async-start | bytes 2097152 | tf_op jit(solution)/shard_map/all_to_all | solution.py:49
  61.5 12.1 %copy-start.1 = (bf16[1,256,1024]{2,1,0:T(8,128)(2,1)S(1)}, bf16[1,256,1024]{2,1,0:T(8,128)(2,1)}, u32[]{:S(2)}) copy-start(bf16[1,256,1024]{2,1,0:T(8,128)(2,1)} %param.5) | copy-start | bytes 1572868
  67.1 6.5 %collective-permute-start.7 = (bf16[2,8,64,512]{3,2,1,0:T(8,128)(2,1)S(1)}, bf16[2,8,64,512]{3,2,1,0:T(8,128)(2,1)S(1)}, u32[]{:S(2)}, u32[]{:S(2)}) collective-permute-start(bf16[2,8,64,512]{3,2,1,0:T(8,128)(2,1)S(1)} %get-tuple-element.8), channel_id=1, source_target_pairs={{0,1},{1,0},{2,3},{3,2},{4,5},{5,4},{6,7},{7,6},{8,9},{9,8},{10,11... | collective-permute-start | bytes 3145736 | tf_op jit(solution)/shard_map/ppermute | solution.py:44
  69.6 51.0 %collective-permute-start.2 = (bf16[256,2048]{1,0:T(8,128)(2,1)S(1)}, bf16[256,2048]{1,0:T(8,128)(2,1)S(1)}, u32[]{:S(2)}, u32[]{:S(2)}) collective-permute-start(bf16[256,2048]{1,0:T(8,128)(2,1)S(1)} %slice.12), channel_id=1, source_target_pairs={{0,64},{64,128},{128,192},{192,256},{256,320},{320,384},{384,448},... | collective-permute-start | bytes 3145736 | tf_op jit(solution)/shard_map/ppermute | solution.py:34
  77.9 52.4 %collective-permute-start.8 = (bf16[256,1024]{1,0:T(8,128)(2,1)S(1)}, bf16[256,1024]{1,0:T(8,128)(2,1)}, u32[]{:S(2)}, u32[]{:S(2)}) collective-permute-start(bf16[256,1024]{1,0:T(8,128)(2,1)S(1)} %attend_b.2), channel_id=1, source_target_pairs={{0,64},{64,128},{128,192},{192,256},{256,320},{320,384},{384,448},... | collective-permute-start | bytes 1572872 | tf_op jit(solution)/shard_map/ppermute | solution.py:34
  81.9 38.7 %collective-permute-start.3 = (bf16[256,512]{1,0:T(8,128)(2,1)S(1)}, bf16[256,512]{1,0:T(8,128)(2,1)S(1)}, u32[]{:S(2)}, u32[]{:S(2)}) collective-permute-start(bf16[256,512]{1,0:T(8,128)(2,1)S(1)} %pad_maximum_fusion), channel_id=1, source_target_pairs={{0,64},{64,128},{128,192},{192,256},{256,320},{320,384},{384,448},... | collective-permute-start | bytes 786440 | tf_op jit(solution)/shard_map/ppermute | solution.py:34
  90.2 42.0 %collective-permute-start.9 = (bf16[256,1024]{1,0:T(8,128)(2,1)S(1)}, bf16[256,1024]{1,0:T(8,128)(2,1)}, u32[]{:S(2)}, u32[]{:S(2)}) collective-permute-start(bf16[256,1024]{1,0:T(8,128)(2,1)S(1)} %attend_b.3), channel_id=1, source_target_pairs={{0,64},{64,128},{128,192},{192,256},{256,320},{320,384},{384,448},... | collective-permute-start | bytes 1572872 | tf_op jit(solution)/shard_map/ppermute | solution.py:34
  120.6 1.0 copy-start.3
  121.6 1.2 copy-start.4
